TPU v7x, 32 devices: a whole 2x2x4 slice. The times are simulated.
32 devices in a mesh: fsdp: 8 (over y, x, core), tp: 4 (over z).
Axes of the slice: x: 2, y: 2, z: 4, core: 2. Of those that a mesh axis runs over, the one named last changes fastest.
Arguments:
- pool: bfloat16 [1024, 16384], P(None, 'fsdp'), may hold values from -6 to 6
- ids: int32 [2, 384], replicated, may hold values from 0 to 1023, as said below
- gate_q: bfloat16 [26624, 16384], P(('fsdp', 'tp')), may hold values from -240 to 240, as said below
- up_q: bfloat16 [26624, 16384], P(('fsdp', 'tp')), may hold values from -240 to 240, as said below
- gate_scale: float32 [208, 128], replicated, may hold values from 3e-05 to 0.0003
- up_scale: float32 [208, 128], replicated, may hold values from 3e-05 to 0.0003
- down_weight: bfloat16 [26624, 16384], P('tp', 'fsdp'), may hold values from -0.0390625 to 0.0390625
Outputs:
- mixed: bfloat16 [2, 384, 16384], P(None, 'tp', 'fsdp')
Inputs may be any that keep to these rules, and one draw needn't show every extreme that they name: All 768 ids are different: no request is decoded twice. `gate_q`: every entry is a value of the 8-bit float form e4m3: a sign times (1 + k / 8) times 2 to the power e, with whole k of 0 to 7 and whole e of 0 to 7. `up_q`: every entry is a value of the 8-bit float form e4m3: a sign times (1 + k / 8) times 2 to the power e, with whole k of 0 to 7 and whole e of 0 to 7.
All inputs are finite; a program needn't handle non-finite values.
Results may differ from a plain program's by a relative error of at most 0.0065.
Values may be sent and summed in bfloat16 or wider, within the bound.
No kernel may reach another device: no remote copies, remote signals or barrier semaphores. Data moves between devices by JAX's collectives and lax.ppermute only.
A program may use at most 448 MiB of HBM per device.

v0:
```python
import jax
import jax.numpy as jnp
from jax import lax
from jax.sharding import PartitionSpec as P

BLOCK = 128


def broadcast(block, axis, owner):
    block = jnp.where(lax.axis_index(axis) == owner, block, jnp.zeros_like(block))
    return lax.psum(block, axis)


def project(hidden, down_weight):
    summed = lax.psum_scatter(
        jnp.dot(hidden, down_weight, preferred_element_type=jnp.float32),
        "tp",
        scatter_dimension=0,
        tiled=True,
    )
    return summed.astype(jnp.bfloat16)


def on_device(pool, ids, gate_q, up_q, gate_scale, up_scale, down_weight):
    n_fsdp = lax.axis_size("fsdp")
    n_tp = lax.axis_size("tp")
    fsdp_index = lax.axis_index("fsdp")
    tp_index = lax.axis_index("tp")
    scales = jnp.stack([gate_scale, up_scale])
    steps = ids.shape[0]
    results = []
    quant = jnp.stack([gate_q, up_q])
    rows_here = quant.shape[1]
    width = quant.shape[2]
    owner = fsdp_index * n_tp + tp_index
    row_blocks = (owner * rows_here + jnp.arange(rows_here, dtype=jnp.int32)) // BLOCK
    row_scales = jnp.take(scales, row_blocks, axis=1)
    weights = (
        (
            quant.astype(jnp.float32).reshape(2, rows_here, width // BLOCK, BLOCK)
            * row_scales[:, :, :, None]
        )
        .astype(jnp.bfloat16)
        .reshape(2, rows_here, width)
    )
    group = n_fsdp // n_tp
    for step in range(steps):
        tokens = jnp.take(pool, ids[step], axis=0)
        columns = weights
        both = jnp.einsum(
            "rd,gfd->rgf",
            lax.all_gather(tokens, "fsdp", axis=1, tiled=True),
            columns,
            preferred_element_type=jnp.float32,
        )
        hidden_own = (jax.nn.silu(both[:, 0]) * both[:, 1]).astype(jnp.bfloat16)
        grouped = lax.all_gather(hidden_own, "tp", axis=1, tiled=True)
        columns = []
        for member in range(group):
            columns.append(broadcast(grouped, "fsdp", group * tp_index + member))
        hidden = jnp.concatenate(columns, axis=1)
        results.append(project(hidden, down_weight))
    return jnp.stack(results)


def solution(mesh):
    in_specs = (
        P(None, "fsdp"),
        P(),
        P(("fsdp", "tp"), None),
        P(("fsdp", "tp"), None),
        P(),
        P(),
        P("tp", "fsdp"),
    )
    out_specs = P(None, "tp", "fsdp")
    return jax.shard_map(
        on_device, mesh=mesh, in_specs=in_specs, out_specs=out_specs, check_vma=False
    )
```

profile of v0, /device:TPU:0, one launch (start us, length us, event | category | flops | bytes accessed | tf_op | source)
XLA Modules:
  0.0 666.3 jit_solution(9128246473485798060)
XLA Ops:
  6.5 0.0 all-gather.5.cloned.1.call-start
  6.5 0.8 slice_reduce_fusion.1
  7.4 7.1 %gather_fusion.1 = bf16[384,2048]{1,0:T(8,128)(2,1)S(1)} fusion(bf16[1024,2048]{1,0:T(8,128)(2,1)} %param.9, s32[1024]{0:T(1024)S(1)} %pad_clamp_fusion.2), kind=kCustom, calls=%fused_computation.clone | custom fusion | bytes 3147264 | tf_op jit(solution)/shard_map/jit(_take)/gather | solution.py:48
  14.5 1.4 broadcast_select_fusion.5
  15.9 0.0 all-gather.5.cloned.1.call-update
  15.9 0.0 all-gather.9.cloned.1.call-start
  16.0 7.1 %gather_fusion.2 = bf16[384,2048]{1,0:T(8,128)(2,1)S(1)} fusion(bf16[1024,2048]{1,0:T(8,128)(2,1)} %param.9, s32[1024]{0:T(1024)S(1)} %pad_clamp_fusion), kind=kCustom, calls=%fused_computation.1.clone | custom fusion | bytes 3147264 | tf_op jit(solution)/shard_map/jit(_take)/gather | solution.py:48
  23.1 0.0 copy-start
  23.1 0.0 copy-start.1
  23.1 1.4 broadcast_select_fusion.4
  24.5 0.0 all-gather.9.cloned.1.call-update
  24.5 0.2 all-gather.7.cloned.1.call-start
  24.8 0.0 copy-done
  24.8 0.0 copy-done.1
  24.9 0.2 pad_maximum_fusion.1
  25.1 3.5 gather_fusion
  28.6 3.1 select_bitcast_fusion
  31.7 0.1 copy.8
  31.7 37.6 %mul.39 = f32[2,832,128,128]{3,2,1,0:T(8,128)} broadcast(f32[2,832,128]{2,1,0:T(8,128)S(1)} %copy.8), dimensions={0,1,2} | broadcast | bytes 109903872 | tf_op jit(solution)/shard_map/mul | solution.py:40
  69.3 116.0 %mul.40 = f32[2,832,16384]{2,1,0:T(8,128)} reshape(f32[2,832,128,128]{3,2,1,0:T(8,128)} %mul.39) | data formatting | bytes 218103808 | tf_op jit(solution)/shard_map/mul | solution.py:40
  185.2 0.0 all-gather.5.cloned.1.call-done
  185.2 60.5 %fusion.2 = f32[384,2,832]{0,2,1:T(8,128)S(1)} fusion(bf16[384,16384]{1,0:T(8,128)(2,1)} %all-gather.5.cloned.1.call-done, f32[2,832,16384]{2,1,0:T(8,128)} %mul.40, bf16[1,832,16384]{2,1,0:T(8,128)(2,1)} %bitcast.42, bf16[1,832,16384]{2,1,0:T(8,128)(2,1)} %bitcast.44), kind=kOutput, calls=%fused_computation.6 | convolution fusion | flops 21101543424 | bytes 178716672 | tf_op jit(solution)/shard_map/rd,gfd->rgf/dot_general | solution.py:50
  245.7 1.2 fusion.15
  247.0 0.0 all-gather.7.cloned.1.call-update
  247.0 0.0 all-gather.11.cloned.1.call-start
  247.0 0.0 all-gather.9.cloned.1.call-done
  247.1 61.2 %fusion = f32[384,2,832]{0,2,1:T(8,128)S(1)} fusion(bf16[384,16384]{1,0:T(8,128)(2,1)} %all-gather.9.cloned.1.call-done, f32[2,832,16384]{2,1,0:T(8,128)} %mul.40, bf16[1,832,16384]{2,1,0:T(8,128)(2,1)} %bitcast.43, bf16[1,832,16384]{2,1,0:T(8,128)(2,1)} %bitcast.45), kind=kOutput, calls=%fused_computation.4 | convolution fusion | flops 21101543424 | bytes 178716672 | tf_op jit(solution)/shard_map/rd,gfd->rgf/dot_general | solution.py:50
  308.2 1.2 fusion.13
  309.4 0.0 all-gather.11.cloned.1.call-update
  309.5 0.3 all-reduce.3.cloned.1.call-start
  309.7 0.0 all-gather.7.cloned.1.call-done
  309.8 4.5 broadcast_select_fusion.3
  314.3 51.8 %all-gather.11.cloned.1.call-done = bf16[384,3328]{0,1:T(8,128)(2,1)} async-done(((bf16[384,832]{0,1:T(8,128)(2,1)}), bf16[384,3328]{0,1:T(8,128)(2,1)}) %all-gather.11.cloned.1.call-update) | async-done | bytes 2555920 | tf_op jit(solution)/shard_map/all_gather | solution.py:57
  366.0 4.4 broadcast_select_fusion.2
  370.4 0.0 all-reduce.3.cloned.1.call-update
  370.4 0.0 reduce-scatter.3.cloned.1.call-start
  370.5 145.1 %all-reduce.3.cloned.1.call-done = (bf16[384,3328]{0,1:T(8,128)(2,1)}, bf16[384,3328]{0,1:T(8,128)(2,1)}, bf16[384,3328]{0,1:T(8,128)(2,1)}, bf16[384,3328]{0,1:T(8,128)(2,1)}) async-done(((bf16[384,3328]{0,1:T(8,128)(2,1)}, bf16[384,3328]{0,1:T(8,128)(2,1)}, bf16[384,3328]{0,1:T(8,128)(2,1)}, bf16[384,3328]{0,1:T(8,128)(2,1)}), (bf16[384,3328]{0,1:T(8,128)(2,1)}, bf16[384,3328]{0,1:T(8,128)(2,1)}, ...) | async-done | bytes 10223632 | tf_op jit(solution)/shard_map/psum | solution.py:11
  515.6 18.4 %fusion.4 = f32[384,2048]{1,0:T(8,128)} fusion(bf16[6656,2048]{1,0:T(8,128)(2,1)} %param.15, bf16[384,3328]{0,1:T(8,128)(2,1)} %get-tuple-element.10, bf16[384,3328]{0,1:T(8,128)(2,1)} %get-tuple-element.11), kind=kOutput, calls=%fused_computation.8 | convolution fusion | flops 10479206400 | bytes 35520512 | tf_op jit(solution)/shard_map/dot_general | solution.py:16
  534.0 0.0 reduce-scatter.3.cloned.1.call-update
  534.0 0.0 reduce-scatter.5.cloned.1.call-start
  534.1 1.6 copy-done.2
  535.7 18.3 %fusion.8 = f32[384,2048]{1,0:T(8,128)} fusion(bf16[6656,2048]{1,0:T(8,128)(2,1)} %param.15, bf16[384,3328]{0,1:T(8,128)(2,1)S(1)} %copy-done.2, bf16[384,3328]{0,1:T(8,128)(2,1)} %get-tuple-element.9), kind=kOutput, calls=%fused_computation.12 | convolution fusion | flops 10479206400 | bytes 35520512 | tf_op jit(solution)/shard_map/dot_general | solution.py:16
  554.0 0.0 reduce-scatter.5.cloned.1.call-update
  554.0 40.6 %reduce-scatter.3.cloned.1.call-done = f32[96,2048]{1,0:T(8,128)} async-done(((f32[384,2048]{1,0:T(8,128)}), f32[96,2048]{1,0:T(8,128)}) %reduce-scatter.3.cloned.1.call-update) | async-done | bytes 786448 | tf_op jit(solution)/shard_map/reduce_scatter | solution.py:15
  594.7 1.2 convert_bitcast_fusion.1
  595.9 61.5 %reduce-scatter.5.cloned.1.call-done = f32[96,2048]{1,0:T(8,128)} async-done(((f32[384,2048]{1,0:T(8,128)}), f32[96,2048]{1,0:T(8,128)}) %reduce-scatter.5.cloned.1.call-update) | async-done | bytes 786448 | tf_op jit(solution)/shard_map/reduce_scatter | solution.py:15
  657.3 1.2 convert_bitcast_fusion
  658.5 0.9 pad_maximum_fusion
  (10 shorter events, 0.1 us)
Async XLA Ops:
  6.5 178.7 %all-gather.5.cloned.1.call-start = ((), (), s32[]{:S(2)}) async-start(), calls=%async_computation.2 | async-start | bytes 14155776 | tf_op jit(solution)/shard_map/all_gather | solution.py:52
  15.9 231.2 %all-gather.9.cloned.1.call-start = ((), (), s32[]{:S(2)}) async-start(), calls=%async_computation.5 | async-start | bytes 14155776 | tf_op jit(solution)/shard_map/all_gather | solution.py:52
  23.1 1.8 copy-start
  23.1 1.7 copy-start.1
  24.5 285.2 %all-gather.7.cloned.1.call-start = ((), (), s32[]{:S(2)}) async-start(), calls=%async_computation.3 | async-start | bytes 3194880 | tf_op jit(solution)/shard_map/all_gather | solution.py:57
  247.0 119.0 %all-gather.11.cloned.1.call-start = ((), (), s32[]{:S(2)}) async-start(), calls=%async_computation.6 | async-start | bytes 3194880 | tf_op jit(solution)/shard_map/all_gather | solution.py:57
  309.5 206.2 %all-reduce.3.cloned.1.call-start = ((), (), s32[]{:S(2)}) async-start(), calls=%async_computation.8 | async-start | bytes 20447232 | tf_op jit(solution)/shard_map/psum | solution.py:11
  370.4 224.2 %reduce-scatter.3.cloned.1.call-start = ((), (), s32[]{:S(2)}) async-start(), calls=%async_computation.4 | async-start | bytes 3932160 | tf_op jit(solution)/shard_map/reduce_scatter | solution.py:15
  534.0 1.7 copy-start.2
  534.0 123.3 %reduce-scatter.5.cloned.1.call-start = ((), (), s32[]{:S(2)}) async-start(), calls=%async_computation.7 | async-start | bytes 3932160 | tf_op jit(solution)/shard_map/reduce_scatter | solution.py:15
Sparse Core Ops, SparseCore 0:
  16.0 74.7 all-gather.4
  92.7 71.9 all-gather.8
  247.1 56.3 all-gather.6
  309.6 56.3 all-gather.10
  370.6 144.9 all-reduce.2
  534.2 60.4 reduce-scatter.2
  597.0 60.3 reduce-scatter.4
where the time goes:
time: 670 us; the launch traced here: 666 us
  waiting for transfers between devices  299 us (45%)
  local copies, waits for them, and re-layouts  174 us (26%)
  matrix products  158 us (24%)
  other arithmetic  20.7 us (3%)
  between operations  13.7 us (2%)
    mul x2, local copies, waits for them, and re-layouts, on_device(): quant.astype(jnp.float32).reshape(2, rows_here, width // BLOCK, BLOCK)  154 us
    psum x1, waiting for transfers between devices, broadcast(): return lax.psum(block, axis)  145 us
    dot_general x2, matrix products, on_device(): jnp.einsum('rd,gfd->rgf', lax.all_gather(tokens, 'fsdp', axis=1, tiled=Tr...  122 us
    reduce_scatter x2, waiting for transfers between devices, project(): lax.psum_scatter(jnp.dot(hidden, down_weight, preferred_element_type=jnp....  102 us
    all_gather x2, waiting for transfers between devices, on_device(): grouped = lax.all_gather(hidden_own, 'tp', axis=1, tiled=True)  51.8 us
    dot_general x2, matrix products, project(): jnp.dot(hidden, down_weight, preferred_element_type=jnp.float32)  36.7 us
    gather x2, local copies, waits for them, and re-layouts, on_device(): tokens = jnp.take(pool, ids[step], axis=0)  14.2 us
  transfers between devices with their start and end apart: 7, of which 4 were waited for; matrix products, arithmetic and copies ran while one was open for 48% of the time, Pallas kernels for 0%

commit v1 on v0

--- a/solution.py
+++ b/solution.py
@@ -6,9 +6,15 @@
 BLOCK = 128
 
 
+def gather_and_add(x, axis):
+    pieces = lax.all_gather(x, axis, axis=0, tiled=False)
+    result = pieces.sum(axis=0)
+    return result
+
+
 def broadcast(block, axis, owner):
     block = jnp.where(lax.axis_index(axis) == owner, block, jnp.zeros_like(block))
-    return lax.psum(block, axis)
+    return gather_and_add(block, axis)
 
 
 def project(hidden, down_weight):

time: 670 us -> 960 us (1.43)
  waiting for transfers between devices: 299 us -> 438 us
  local copies, waits for them, and re-layouts: 174 us -> 252 us
  other arithmetic: 20.7 us -> 78 us
  matrix products: 158 us -> 168 us
    all_gather x0 -> x4, waiting for transfers between devices: none -> 325 us  [gather_and_add(): pieces = lax.all_gather(x, axis, axis=0, tiled=False)]
    psum x1 -> x0, waiting for transfers between devices: 145 us -> none  [broadcast(): return lax.psum(block, axis)]
    unnamed x6 -> x12, local copies, waits for them, and re-layouts: 1.66 us -> 80.3 us
    reduce_sum x0 -> x2, other arithmetic: none -> 57.4 us  [gather_and_add(): result = pieces.sum(axis=0)]
    reduce_scatter x2, waiting for transfers between devices: 102 us -> 59.5 us  [project(): lax.psum_scatter(jnp.dot(hidden, down_weight, preferred_element_type=jnp....]
    dot_general x2, matrix products: 36.7 us -> 46.6 us  [project(): jnp.dot(hidden, down_weight, preferred_element_type=jnp.float32)]
  transfers between devices with their start and end apart: 7 -> 10, of which waited for: 4 -> 6; matrix products, arithmetic and copies ran while one was open for 48% -> 51% of each run, Pallas kernels for 0% -> 0%
where the time goes in v1:
time: 960 us; the launch traced here: 952 us
  waiting for transfers between devices  438 us (46%)
  local copies, waits for them, and re-layouts  252 us (26%)
  matrix products  168 us (18%)
  other arithmetic  78 us (8%)
  between operations  14 us (1%)
    all_gather x4, waiting for transfers between devices, gather_and_add(): pieces = lax.all_gather(x, axis, axis=0, tiled=False)  325 us
    mul x2, local copies, waits for them, and re-layouts, on_device(): quant.astype(jnp.float32).reshape(2, rows_here, width // BLOCK, BLOCK)  153 us
    dot_general x2, matrix products, on_device(): jnp.einsum('rd,gfd->rgf', lax.all_gather(tokens, 'fsdp', axis=1, tiled=Tr...  122 us
    unnamed x12, local copies, waits for them, and re-layouts  80.3 us
    reduce_scatter x2, waiting for transfers between devices, project(): lax.psum_scatter(jnp.dot(hidden, down_weight, preferred_element_type=jnp....  59.5 us
    reduce_sum x2, other arithmetic, gather_and_add(): result = pieces.sum(axis=0)  57.4 us
    all_gather x2, waiting for transfers between devices, on_device(): grouped = lax.all_gather(hidden_own, 'tp', axis=1, tiled=True)  51.4 us
    dot_general x2, matrix products, project(): jnp.dot(hidden, down_weight, preferred_element_type=jnp.float32)  46.6 us
  transfers between devices with their start and end apart: 10, of which 6 were waited for; matrix products, arithmetic and copies ran while one was open for 51% of the time, Pallas kernels for 0%

profile of v1, /device:TPU:0, one launch (start us, length us, event | category | flops | bytes accessed | tf_op | source)
XLA Modules:
  0.0 951.5 jit_solution(7174265848508875846)
XLA Ops:
  6.5 0.8 slice_reduce_fusion.1
  7.4 7.1 gather_fusion.1
  14.5 1.4 broadcast_select_fusion.5
  15.9 0.0 all-gather.17.cloned.1.call-start
  15.9 7.1 gather_fusion.2
  23.1 1.4 broadcast_select_fusion.4
  24.5 0.5 all-gather.15.cloned.1.call-start
  25.1 0.2 pad_maximum_fusion.1
  25.3 3.5 gather_fusion
  28.9 3.1 select_bitcast_fusion
  31.9 0.1 copy.9
  32.0 37.6 %mul.39 = f32[2,832,128,128]{3,2,1,0:T(8,128)} broadcast(f32[2,832,128]{2,1,0:T(8,128)S(1)} %copy.9), dimensions={0,1,2} | broadcast | bytes 109903872 | tf_op jit(solution)/shard_map/mul | solution.py:46
  69.5 115.9 %mul.40 = f32[2,832,16384]{2,1,0:T(8,128)} reshape(f32[2,832,128,128]{3,2,1,0:T(8,128)} %mul.39) | data formatting | bytes 218103808 | tf_op jit(solution)/shard_map/mul | solution.py:46
  185.4 60.5 %fusion.2 = f32[384,2,832]{0,2,1:T(8,128)S(1)} fusion(bf16[384,16384]{1,0:T(8,128)(2,1)} %all-gather.13.cloned.1.call-done, f32[2,832,16384]{2,1,0:T(8,128)} %mul.40, bf16[1,832,16384]{2,1,0:T(8,128)(2,1)} %bitcast.66, bf16[1,832,16384]{2,1,0:T(8,128)(2,1)} %bitcast.68), kind=kOutput, calls=%fused_computation.10 | convolution fusion | flops 21101543424 | bytes 178716672 | tf_op jit(solution)/shard_map/rd,gfd->rgf/dot_general | solution.py:56
  245.9 1.2 fusion.15
  247.1 0.0 all-gather.19.cloned.1.call-start
  247.1 0.0 all-gather.17.cloned.1.call-done
  247.2 61.2 %fusion = f32[384,2,832]{0,2,1:T(8,128)S(1)} fusion(bf16[384,16384]{1,0:T(8,128)(2,1)} %all-gather.17.cloned.1.call-done, f32[2,832,16384]{2,1,0:T(8,128)} %mul.40, bf16[1,832,16384]{2,1,0:T(8,128)(2,1)} %bitcast.67, bf16[1,832,16384]{2,1,0:T(8,128)(2,1)} %bitcast.69), kind=kOutput, calls=%fused_computation.8 | convolution fusion | flops 21101543424 | bytes 178716672 | tf_op jit(solution)/shard_map/rd,gfd->rgf/dot_general | solution.py:56
  308.4 1.2 fusion.13
  309.6 0.2 all-gather.21.cloned.1.call-start
  309.8 4.5 broadcast_select_fusion.3
  314.3 0.0 all-gather.23.cloned.1.call-start
  314.4 0.5 all-gather.23.cloned.1.call-update
  314.9 0.0 all-gather.25.cloned.1.call-start
  314.9 51.4 %all-gather.19.cloned.1.call-done = bf16[384,3328]{0,1:T(8,128)(2,1)} async-done(((bf16[384,832]{0,1:T(8,128)(2,1)}), bf16[384,3328]{0,1:T(8,128)(2,1)}) %all-gather.19.cloned.1.call-update) | async-done | bytes 2555920 | tf_op jit(solution)/shard_map/all_gather | solution.py:63
  366.3 4.4 broadcast_select_fusion.2
  370.7 0.0 all-gather.27.cloned.1.call-start
  370.8 0.7 all-gather.27.cloned.1.call-update
  371.5 0.0 reduce-scatter.3.cloned.1.call-start
  371.5 104.6 %all-gather.21.cloned.1.call-done = bf16[3072,3328]{0,1:T(8,128)(2,1)} async-done(((bf16[384,3328]{0,1:T(8,128)(2,1)}), bf16[3072,3328]{0,1:T(8,128)(2,1)}) %all-gather.21.cloned.1.call-update) | async-done | bytes 20447248 | tf_op jit(solution)/shard_map/all_gather | solution.py:10
  476.1 19.0 %copy.10 = bf16[416,8,8,384]{3,2,1,0:T(8,128)(2,1)} copy(bf16[416,8,8,384]{3,1,2,0:T(8,128)(2,1)} %bitcast.60) | data formatting | bytes 40894464
  495.2 92.0 %all-gather.23.cloned.1.call-done = bf16[3072,3328]{0,1:T(8,128)(2,1)} async-done(((bf16[384,3328]{0,1:T(8,128)(2,1)}), bf16[3072,3328]{0,1:T(8,128)(2,1)}) %all-gather.23.cloned.1.call-update) | async-done | bytes 20447248 | tf_op jit(solution)/shard_map/all_gather | solution.py:10
  587.2 20.9 %copy.11 = bf16[416,8,8,384]{3,2,1,0:T(8,128)(2,1)} copy(bf16[416,8,8,384]{3,1,2,0:T(8,128)(2,1)} %bitcast.62) | data formatting | bytes 40894464
  608.1 1.0 copy-done
  609.1 28.7 %bitcast_reduce_fusion.2 = (bf16[384,3328]{0,1:T(8,128)(2,1)S(1)}, bf16[384,3328]{0,1:T(8,128)(2,1)S(1)}) fusion(bf16[416,8,8,384]{3,2,1,0:T(8,128)(2,1)} %copy.11, bf16[416,8,8,384]{3,2,1,0:T(8,128)(2,1)S(1)} %copy-done), kind=kLoop, calls=%fused_computation.6 | loop fusion | flops 17891328 | bytes 46006272 | tf_op jit(solution)/shard_map/reduce_sum | solution.py:11
  637.8 23.5 %fusion.4 = f32[384,2048]{1,0:T(8,128)} fusion(bf16[6656,2048]{1,0:T(8,128)(2,1)} %param.15, bf16[384,3328]{0,1:T(8,128)(2,1)S(1)} %get-tuple-element.14, bf16[384,3328]{0,1:T(8,128)(2,1)S(1)} %get-tuple-element.15), kind=kOutput, calls=%fused_computation.12 | convolution fusion | flops 10479206400 | bytes 35520512 | tf_op jit(solution)/shard_map/dot_general | solution.py:22
  661.3 0.3 reduce-scatter.5.cloned.1.call-start
  661.6 36.8 %all-gather.25.cloned.1.call-done = bf16[3072,3328]{0,1:T(8,128)(2,1)} async-done(((bf16[384,3328]{0,1:T(8,128)(2,1)}), bf16[3072,3328]{0,1:T(8,128)(2,1)}) %all-gather.25.cloned.1.call-update) | async-done | bytes 20447248 | tf_op jit(solution)/shard_map/all_gather | solution.py:10
  698.3 19.1 %copy.12 = bf16[416,8,8,384]{3,2,1,0:T(8,128)(2,1)} copy(bf16[416,8,8,384]{3,1,2,0:T(8,128)(2,1)} %bitcast.61) | data formatting | bytes 40894464
  717.4 92.1 %all-gather.27.cloned.1.call-done = bf16[3072,3328]{0,1:T(8,128)(2,1)} async-done(((bf16[384,3328]{0,1:T(8,128)(2,1)}), bf16[3072,3328]{0,1:T(8,128)(2,1)}) %all-gather.27.cloned.1.call-update) | async-done | bytes 20447248 | tf_op jit(solution)/shard_map/all_gather | solution.py:10
  809.5 20.3 %copy.13 = bf16[416,8,8,384]{3,2,1,0:T(8,128)(2,1)} copy(bf16[416,8,8,384]{3,1,2,0:T(8,128)(2,1)} %bitcast.63) | data formatting | bytes 40894464
  829.8 28.7 %bitcast_reduce_fusion = (bf16[384,3328]{0,1:T(8,128)(2,1)S(1)}, bf16[384,3328]{0,1:T(8,128)(2,1)S(1)}) fusion(bf16[416,8,8,384]{3,2,1,0:T(8,128)(2,1)} %copy.13, bf16[416,8,8,384]{3,2,1,0:T(8,128)(2,1)S(1)} %copy-done.1), kind=kLoop, calls=%fused_computation.4 | loop fusion | flops 17891328 | bytes 46006272 | tf_op jit(solution)/shard_map/reduce_sum | solution.py:11
  858.5 23.1 %fusion.8 = f32[384,2048]{1,0:T(8,128)} fusion(bf16[6656,2048]{1,0:T(8,128)(2,1)} %param.15, bf16[384,3328]{0,1:T(8,128)(2,1)S(1)} %get-tuple-element.12, bf16[384,3328]{0,1:T(8,128)(2,1)S(1)} %get-tuple-element.13), kind=kOutput, calls=%fused_computation.16 | convolution fusion | flops 10479206400 | bytes 35520512 | tf_op jit(solution)/shard_map/dot_general | solution.py:22
  881.6 0.0 reduce-scatter.3.cloned.1.call-done
  881.7 1.2 convert_bitcast_fusion.1
  882.8 59.5 %reduce-scatter.5.cloned.1.call-done = f32[96,2048]{1,0:T(8,128)} async-done(((f32[384,2048]{1,0:T(8,128)}), f32[96,2048]{1,0:T(8,128)}) %reduce-scatter.5.cloned.1.call-update) | async-done | bytes 786448 | tf_op jit(solution)/shard_map/reduce_scatter | solution.py:21
  942.3 1.2 convert_bitcast_fusion
  943.5 0.9 pad_maximum_fusion
  (27 shorter events, 0.3 us)
Async XLA Ops:
  6.5 178.9 %all-gather.13.cloned.1.call-start = ((), (), s32[]{:S(2)}) async-start(), calls=%async_computation.2 | async-start | bytes 14155776 | tf_op jit(solution)/shard_map/all_gather | solution.py:58
  15.9 231.3 %all-gather.17.cloned.1.call-start = ((), (), s32[]{:S(2)}) async-start(), calls=%async_computation.5 | async-start | bytes 14155776 | tf_op jit(solution)/shard_map/all_gather | solution.py:58
  23.1 2.0 copy-start.2
  23.1 2.0 copy-start.3
  24.5 285.3 %all-gather.15.cloned.1.call-start = ((), (), s32[]{:S(2)}) async-start(), calls=%async_computation.3 | async-start | bytes 3194880 | tf_op jit(solution)/shard_map/all_gather | solution.py:63
  247.1 119.2 %all-gather.19.cloned.1.call-start = ((), (), s32[]{:S(2)}) async-start(), calls=%async_computation.6 | async-start | bytes 3194880 | tf_op jit(solution)/shard_map/all_gather | solution.py:63
  309.6 166.6 %all-gather.21.cloned.1.call-start = ((), (), s32[]{:S(2)}) async-start(), calls=%async_computation.8 | async-start | bytes 23003136 | tf_op jit(solution)/shard_map/all_gather | solution.py:10
  314.3 272.9 %all-gather.23.cloned.1.call-start = ((), (), s32[]{:S(2)}) async-start(), calls=%async_computation.9 | async-start | bytes 23003136 | tf_op jit(solution)/shard_map/all_gather | solution.py:10
  314.9 383.4 %all-gather.25.cloned.1.call-start = ((), (), s32[]{:S(2)}) async-start(), calls=%async_computation.10 | async-start | bytes 23003136 | tf_op jit(solution)/shard_map/all_gather | solution.py:10
  370.7 438.8 %all-gather.27.cloned.1.call-start = ((), (), s32[]{:S(2)}) async-start(), calls=%async_computation.11 | async-start | bytes 23003136 | tf_op jit(solution)/shard_map/all_gather | solution.py:10
  371.5 510.2 %reduce-scatter.3.cloned.1.call-start = ((), (), s32[]{:S(2)}) async-start(), calls=%async_computation.4 | async-start | bytes 3932160 | tf_op jit(solution)/shard_map/reduce_scatter | solution.py:21
  587.2 21.9 %copy-start = (bf16[416,8,8,384]{3,2,1,0:T(8,128)(2,1)S(1)}, bf16[416,8,8,384]{3,2,1,0:T(8,128)(2,1)}, u32[]{:S(2)}) copy-start(bf16[416,8,8,384]{3,2,1,0:T(8,128)(2,1)} %copy.10) | copy-start | bytes 61341700
  661.3 281.0 %reduce-scatter.5.cloned.1.call-start = ((), (), s32[]{:S(2)}) async-start(), calls=%async_computation.7 | async-start | bytes 3932160 | tf_op jit(solution)/shard_map/reduce_scatter | solution.py:21
  809.5 20.3 %copy-start.1 = (bf16[416,8,8,384]{3,2,1,0:T(8,128)(2,1)S(1)}, bf16[416,8,8,384]{3,2,1,0:T(8,128)(2,1)}, u32[]{:S(2)}) copy-start(bf16[416,8,8,384]{3,2,1,0:T(8,128)(2,1)} %copy.12) | copy-start | bytes 61341700
Sparse Core Ops, SparseCore 0:
  16.0 74.7 all-gather.12
  92.6 71.9 all-gather.16
  247.2 56.5 all-gather.14
  309.7 56.5 all-gather.18
  368.0 108.0 all-gather.20
  477.9 109.2 all-gather.22
  589.0 109.2 all-gather.24
  700.2 109.2 all-gather.26
  811.8 60.3 reduce-scatter.2
  881.7 60.5 reduce-scatter.4
